TPU v7x, 512 devices: a whole 4x8x8 slice. The times are simulated.
512 devices in a mesh: src: 16 (over z, core), row: 32 (over x, y).
Axes of the slice: x: 4, y: 8, z: 8, core: 2. Of those that a mesh axis runs over, the one named last changes fastest.
Arguments:
- spec_re: bfloat16 [1024, 1024], P('row'), may hold values from -18 to 18
- spec_im: bfloat16 [1024, 1024], P('row'), may hold values from -18 to 18
- target: float32 [1024, 1024], P('row'), may hold values from 0.3 to 1.5
- weights: float32 [128], P('src'), may hold values from 0.25 to 2.5
- cent_row: int32 [128], P('src'), may hold values from 128 to 895
- cent_col: int32 [128], P('src'), may hold values from 128 to 895
Outputs:
- grad_re: float32 [1024, 1024], P('row')
- grad_im: float32 [1024, 1024], P('row')
Inputs may be any that keep to these rules, and one draw needn't show every extreme that they name: Every pupil disk of radius 128 about (cent_row, cent_col) lies inside the band.
All inputs are finite; a program needn't handle non-finite values.
Results may differ from a plain program's by a relative error of at most 0.0072.
Values may be sent and summed in bfloat16 or wider, within the bound.
No kernel may reach another device: no remote copies, remote signals or barrier semaphores. Data moves between devices by JAX's collectives and lax.ppermute only.
A program may use at most 128 MiB of HBM per device.

v0:
```python
import math
import jax
import jax.numpy as jnp
from jax import lax
from jax.sharding import PartitionSpec as P

RAD = 128
WIN = 384


def make_tables(band):
    position = jnp.arange(band, dtype=jnp.int32)
    phase = position[:, None] * position[None, :] % band
    angle = phase.astype(jnp.float32) * (2.0 * math.pi / band)
    factor = 1.0 / math.sqrt(band)
    return (
        (jnp.cos(angle) * factor).astype(jnp.bfloat16),
        (jnp.sin(angle) * factor).astype(jnp.bfloat16),
    )


def local(spec_re, spec_im, target, weights, cent_row, cent_col):
    rows_dev, band = spec_re.shape
    cols_dev = target.shape[0]
    points_dev = weights.shape[0]
    total_points = points_dev * lax.axis_size("src")
    cosine, sine = make_tables(band)
    tables_joined = jnp.concatenate([cosine, sine], axis=1)
    row_first = lax.axis_index("row") * rows_dev
    window_index = jnp.arange(WIN, dtype=jnp.int32)
    zero_value = jnp.zeros((), jnp.bfloat16)
    stacked = jnp.stack([spec_re, spec_im], axis=0)

    def window_starts(centre_cols):
        return jnp.clip(centre_cols - RAD, 0, band - WIN)

    def disk_window(first_row, row_count, centre_rows, centre_cols, starts):
        rows_here = first_row + jnp.arange(row_count, dtype=jnp.int32)
        row_gap = rows_here[None, :] - centre_rows[:, None]
        col_gap = starts[:, None] + window_index[None, :] - centre_cols[:, None]
        return row_gap[:, :, None] ** 2 + col_gap[:, None, :] ** 2 <= RAD * RAD

    col_first = lax.axis_index("row") * cols_dev
    narrow = jnp.concatenate(
        [
            lax.dynamic_slice_in_dim(cosine, col_first, cols_dev, 1),
            lax.dynamic_slice_in_dim(sine, col_first, cols_dev, 1),
        ],
        axis=1,
    )
    starts_all = window_starts(cent_col)
    narrow_windows = jax.vmap(lambda start: lax.dynamic_slice_in_dim(narrow, start, WIN, 0))(
        starts_all
    )
    spectrum_piece = lax.all_gather(stacked, "row", axis=1, tiled=True)
    inside_disk = disk_window(jnp.int32(0), spectrum_piece.shape[1], cent_row, cent_col, starts_all)
    pieces = jax.vmap(lambda start: lax.dynamic_slice_in_dim(spectrum_piece, start, WIN, 2))(
        starts_all
    )
    masked = jnp.where(inside_disk[:, None], pieces, zero_value)
    product = jnp.einsum(
        "pckl,plz->pckz", masked, narrow_windows, preferred_element_type=jnp.float32
    )
    real_part = product[:, 0, :, :cols_dev] - product[:, 1, :, cols_dev:]
    imag_part = product[:, 0, :, cols_dev:] + product[:, 1, :, :cols_dev]
    received = jnp.stack([real_part, imag_part], axis=1).astype(jnp.bfloat16)
    product = jnp.einsum(
        "pcky,kz->pcyz", received, tables_joined, preferred_element_type=jnp.float32
    )
    field_re = product[:, 0, :, :band] - product[:, 1, :, band:]
    field_im = product[:, 0, :, band:] + product[:, 1, :, :band]
    field = jnp.stack([field_re, field_im], axis=1)
    power = field[:, 0] * field[:, 0] + field[:, 1] * field[:, 1]
    local_power = jnp.sum(weights[:, None, None] * power, axis=0) / total_points
    intensity = lax.psum(local_power, "src")
    mismatch = intensity - target
    grad_field = (2.0 * weights[:, None, None, None] * mismatch[None, None] * field).astype(
        jnp.bfloat16
    )
    product = jnp.einsum(
        "pcyx,xz->pcyz", grad_field, tables_joined, preferred_element_type=jnp.float32
    )
    adj_re = product[:, 0, :, :band] + product[:, 1, :, band:]
    adj_im = product[:, 1, :, :band] - product[:, 0, :, band:]
    adjoint = jnp.stack([adj_re, adj_im], axis=1).astype(jnp.bfloat16)
    returned = lax.all_to_all(adjoint, "row", split_axis=3, concat_axis=2, tiled=True)
    starts = window_starts(cent_col)
    inside_disk = disk_window(row_first, rows_dev, cent_row, cent_col, starts)
    col_tables = jax.vmap(
        lambda start: jnp.concatenate(
            [
                lax.dynamic_slice_in_dim(cosine, start, WIN, 1),
                lax.dynamic_slice_in_dim(sine, start, WIN, 1),
            ],
            axis=1,
        )
    )(starts)
    result = jnp.einsum("pcyk,pyz->pckz", returned, col_tables, preferred_element_type=jnp.float32)
    term_re = result[:, 0, :, :WIN] + result[:, 1, :, WIN:]
    term_im = result[:, 1, :, :WIN] - result[:, 0, :, WIN:]
    zero_float = jnp.zeros((), jnp.float32)
    terms_re = jnp.where(inside_disk, term_re, zero_float)
    terms_im = jnp.where(inside_disk, term_im, zero_float)
    starts_local = window_starts(cent_col)
    local_re = jnp.zeros((rows_dev, band), jnp.float32)
    local_im = jnp.zeros((rows_dev, band), jnp.float32)
    for point in range(points_dev):
        start = starts_local[point]
        old_re = lax.dynamic_slice_in_dim(local_re, start, WIN, 1)
        old_im = lax.dynamic_slice_in_dim(local_im, start, WIN, 1)
        local_re = lax.dynamic_update_slice_in_dim(local_re, old_re + terms_re[point], start, 1)
        local_im = lax.dynamic_update_slice_in_dim(local_im, old_im + terms_im[point], start, 1)
    grad_re, grad_im = lax.psum((local_re, local_im), "src")
    return (grad_re, grad_im)


def solution(mesh):
    return jax.shard_map(
        local,
        mesh=mesh,
        in_specs=(P("row", None), P("row", None), P("row", None), P("src"), P("src"), P("src")),
        out_specs=(P("row", None), P("row", None)),
        check_vma=False,
    )
```

profile of v0, /device:TPU:1, one launch (start us, length us, event | category | flops | bytes accessed | tf_op | source)
XLA Modules:
  0.0 504.2 jit_solution(15990547782452756728)
XLA Ops:
  9.6 15.8 %multiply_convert_fusion = bf16[1024,1024]{1,0:T(8,128)(2,1)S(1)} fusion(), kind=kLoop, calls=%fused_computation.23 | loop fusion | flops 16777216 | bytes 2097152 | tf_op jit(solution)/shard_map/convert_element_type | solution.py:18
  25.4 15.7 %multiply_convert_fusion.1 = bf16[1024,1024]{1,0:T(8,128)(2,1)S(1)} fusion(), kind=kLoop, calls=%fused_computation.24 | loop fusion | flops 16777216 | bytes 2097152 | tf_op jit(solution)/shard_map/convert_element_type | solution.py:17
  45.4 9.7 %while.9 = (s32[]{:T(128)}, bf16[1024,64]{1,0:T(8,128)(2,1)S(1)}, s32[8,2]{0,1:T(2,128)S(1)}, bf16[8,384,64]{2,1,0:T(8,128)(2,1)S(1)}) while((s32[]{:T(128)}, bf16[1024,64]{1,0:T(8,128)(2,1)S(1)}, s32[8,2]{0,1:T(2,128)S(1)}, bf16[8,384,64]{2,1,0:T(8,128)(2,1)S(1)}) %tuple.83), condition=%wide.while_cond.1.clone, body=%wide.while_body.1.sunk.clone | while | flops 2 | bytes 196705 | solution.py:52
  58.2 30.4 %while.11 = (s32[]{:T(128)}, bf16[1024,1024]{1,0:T(8,128)(2,1)}, s32[8,2]{0,1:T(2,128)S(1)}, bf16[8,1024,384]{2,1,0:T(8,128)(2,1)}) while((s32[]{:T(128)}, bf16[1024,1024]{1,0:T(8,128)(2,1)}, s32[8,2]{0,1:T(2,128)S(1)}, bf16[8,1024,384]{2,1,0:T(8,128)(2,1)}) %tuple.100), condition=%wide.while_cond.3.clone, body=%wide.while_body.3.sunk.clone | while | flops 2 | bytes 1573469 | solution.py:93
  88.5 12.4 %all-gather.2.cloned.1.call-done = bf16[2,1024,1024]{2,1,0:T(8,128)(2,1)} async-done(((bf16[2,32,1024]{2,1,0:T(8,128)(2,1)}), bf16[2,1024,1024]{2,1,0:T(8,128)(2,1)}) %all-gather.2.cloned.1.call-update) | async-done | bytes 4194320 | tf_op jit(solution)/shard_map/all_gather | solution.py:55
  101.0 37.9 %while.8 = (s32[]{:T(128)}, bf16[2,1024,1024]{2,1,0:T(8,128)(2,1)}, s32[8,3]{0,1:T(4,128)S(1)}, bf16[8,2,1024,384]{3,2,1,0:T(8,128)(2,1)}) while((s32[]{:T(128)}, bf16[2,1024,1024]{2,1,0:T(8,128)(2,1)}, s32[8,3]{0,1:T(4,128)S(1)}, bf16[8,2,1024,384]{3,2,1,0:T(8,128)(2,1)}) %tuple.80), condition=%wide.while_cond.clone, body=%wide.while_body.sunk.clone | while | flops 2 | bytes 3146341 | solution.py:57
  101.5 4.2 bitcast_dynamic-update-slice_fusion.12
  106.3 4.2 bitcast_dynamic-update-slice_fusion.12
  111.0 4.2 bitcast_dynamic-update-slice_fusion.12
  115.8 4.2 bitcast_dynamic-update-slice_fusion.12
  120.6 4.1 bitcast_dynamic-update-slice_fusion.12
  129.9 4.2 bitcast_dynamic-update-slice_fusion.12
  134.7 4.2 bitcast_dynamic-update-slice_fusion.12
  138.9 7.7 %fusion = f32[8,2,1024,64]{2,3,1,0:T(8,128)S(1)} fusion(bf16[8,2,1024,384]{3,2,1,0:T(8,128)(2,1)} %get-tuple-element.9, pred[8,1024,384]{2,1,0:T(8,128)(4,1)} %add_compare_fusion, bf16[8,384,64]{2,1,0:T(8,128)(2,1)S(1)} %get-tuple-element.17), kind=kOutput, calls=%fused_computation.9 | convolution fusion | flops 811597824 | bytes 20316160 | tf_op jit(solution)/shard_map/pckl,plz->pckz/dot_general | solution.py:61
  152.9 116.9 %all-reduce.7.cloned.1.call-done = f32[32,1024]{1,0:T(8,128)} async-done(((f32[32,1024]{1,0:T(8,128)}), f32[32,1024]{1,0:T(8,128)}) %all-reduce.7.cloned.1.call-update) | async-done | bytes 131088 | tf_op jit(solution)/shard_map/psum | solution.py:75
  270.9 4.3 fusion.11
  275.6 7.5 %copy.13 = bf16[8,2,32,1024]{2,1,0,3:T(2,128)(2,1)} copy(bf16[8,2,32,1024]{3,2,1,0:T(8,128)(2,1)S(1)} %pad_maximum_fusion) | data formatting | bytes 2097152 | tf_op jit(solution)/shard_map/stack | solution.py:85
  283.2 9.9 %reshape.192 = bf16[32,2,8192]{2,1,0:T(2,128)(2,1)} reshape(bf16[1024,8,2,32]{3,2,1,0:T(2,128)(2,1)} %bitcast.159) | data formatting | bytes 2097152
  293.1 9.3 %all-to-all-start = ((bf16[32,2,8192]{2,1,0:T(2,128)(2,1)}), bf16[32,2,8192]{2,1,0:T(2,128)(2,1)S(1)}, u32[]{:S(2)}, u32[]{:S(2)}) async-start(bf16[32,2,8192]{2,1,0:T(2,128)(2,1)} %reshape.192), calls=%async_computation | async-start | bytes 2097152 | tf_op jit(solution)/shard_map/all_to_all | solution.py:86
  321.4 19.9 %while.10 = (s32[]{:T(128)}, bf16[1024,1024]{1,0:T(8,128)(2,1)S(1)}, s32[8,2]{0,1:T(2,128)S(1)}, bf16[8,1024,384]{2,1,0:T(8,128)(2,1)}) while((s32[]{:T(128)}, bf16[1024,1024]{1,0:T(8,128)(2,1)S(1)}, s32[8,2]{0,1:T(2,128)S(1)}, bf16[8,1024,384]{2,1,0:T(8,128)(2,1)}) %tuple.101), condition=%wide.while_cond.2.clone, body=%wide.while_body.2.sunk.clone | while | flops 2 | bytes 1573469 | solution.py:92
  344.8 6.9 %copy.25 = bf16[8,2,32,32,32]{2,3,4,1,0:T(8,128)(2,1)} copy(bf16[8,2,32,32,32]{2,1,0,4,3:T(2,128)(2,1)} %bitcast.160) | data formatting | bytes 2097152 | tf_op jit(solution)/shard_map/all_to_all | solution.py:86
  351.8 6.2 %all_to_all.16 = bf16[8,2,1024,32]{2,3,1,0:T(8,128)(2,1)S(1)} reshape(bf16[8,2,32,32,32]{3,2,4,1,0:T(8,128)(2,1)} %bitcast.161) | data formatting | bytes 2097152 | tf_op jit(solution)/shard_map/all_to_all | solution.py:86
  357.9 5.8 %fusion.2 = f32[8,2,32,768]{3,2,1,0:T(8,128)S(1)} fusion(bf16[8,2,1024,32]{2,3,1,0:T(8,128)(2,1)S(1)} %all_to_all.16, bf16[8,1024,384]{2,1,0:T(8,128)(2,1)} %get-tuple-element.33, bf16[8,1024,384]{2,1,0:T(8,128)(2,1)} %get-tuple-element.25), kind=kOutput, calls=%fused_computation.12 | convolution fusion | flops 830472192 | bytes 15204352 | tf_op jit(solution)/shard_map/pcyk,pyz->pckz/dot_general | solution.py:98
  376.7 117.8 %all-reduce.9.cloned.1.call-done = (f32[32,1024]{1,0:T(8,128)}, f32[32,1024]{1,0:T(8,128)}) async-done(((f32[32,1024]{1,0:T(8,128)}, f32[32,1024]{1,0:T(8,128)}), (f32[32,1024]{1,0:T(8,128)}, f32[32,1024]{1,0:T(8,128)})) %all-reduce.9.cloned.1.call-update) | async-done | bytes 262160 | tf_op jit(solution)/shard_map/psum | solution.py:113
  (175 shorter events, 109.2 us)
Async XLA Ops:
  7.2 34.5 %copy-start.7 = (s32[8]{0:T(128)S(1)}, s32[8]{0:T(128)}, u32[]{:S(2)}) copy-start(s32[8]{0:T(128)} %param.11) | copy-start | bytes 100
  7.2 34.4 %copy-start.5 = (s32[8]{0:T(128)S(1)}, s32[8]{0:T(128)}, u32[]{:S(2)}) copy-start(s32[8]{0:T(128)} %param.10) | copy-start | bytes 100
  7.2 93.8 %all-gather.2.cloned.1.call-start = ((), (), s32[]{:S(2)}) async-start(), calls=%async_computation.1 | async-start | bytes 4325376 | tf_op jit(solution)/shard_map/all_gather | solution.py:55
  8.8 261.0 %all-reduce.7.cloned.1.call-start = ((), (), s32[]{:S(2)}) async-start(), calls=%async_computation.2 | async-start | bytes 262144 | tf_op jit(solution)/shard_map/psum | solution.py:75
  25.4 15.7 %copy-start = (bf16[1024,1024]{1,0:T(8,128)(2,1)}, bf16[1024,1024]{1,0:T(8,128)(2,1)S(1)}, u32[]{:S(2)}) copy-start(bf16[1024,1024]{1,0:T(8,128)(2,1)S(1)} %multiply_convert_fusion) | copy-start | bytes 6291460
  146.6 1.6 copy-start.1
  148.2 2.4 copy-start.6
  150.5 119.3 %copy-start.4 = (f32[32,1024]{1,0:T(8,128)S(1)}, f32[32,1024]{1,0:T(8,128)}, u32[]{:S(2)}) copy-start(f32[32,1024]{1,0:T(8,128)} %param.8) | copy-start | bytes 393220
  293.1 48.2 %all-to-all-start = ((bf16[32,2,8192]{2,1,0:T(2,128)(2,1)}), bf16[32,2,8192]{2,1,0:T(2,128)(2,1)S(1)}, u32[]{:S(2)}, u32[]{:S(2)}) async-start(bf16[32,2,8192]{2,1,0:T(2,128)(2,1)} %reshape.192), calls=%async_computation | async-start | bytes 2097152 | tf_op jit(solution)/shard_map/all_to_all | solution.py:86
  302.4 192.2 %all-reduce.9.cloned.1.call-start = ((), (), s32[]{:S(2)}) async-start(), calls=%async_computation.3 | async-start | bytes 524288 | tf_op jit(solution)/shard_map/psum | solution.py:113
  370.0 6.1 %copy-start.3 = (f32[32,1024]{1,0:T(8,128)}, f32[32,1024]{1,0:T(8,128)S(1)}, u32[]{:S(2)}) copy-start(f32[32,1024]{1,0:T(8,128)S(1)} %dynamic_update_slice.55) | copy-start | bytes 393220
  376.0 0.7 copy-start.2
Sparse Core Ops, SparseCore 0:
  11.7 89.1 all-gather.1
  153.0 116.7 all-reduce.6
  376.8 117.6 all-reduce.8
where the time goes:
time: 506 us; the launch traced here: 504 us
  waiting for transfers between devices  247 us (49%)
  local copies, waits for them, and re-layouts  155 us (31%)
  other arithmetic  43.3 us (9%)
  between operations  29.3 us (6%)
  matrix products  20.2 us (4%)
  starting transfers between devices  9.38 us (2%)
    psum x1, waiting for transfers between devices, local(): grad_re, grad_im = lax.psum((local_re, local_im), 'src')  118 us
    psum x1, waiting for transfers between devices, local(): intensity = lax.psum(local_power, 'src')  117 us
    gather x96, local copies, waits for them, and re-layouts  97.7 us
    unnamed x22, local copies, waits for them, and re-layouts  24.9 us
    convert_element_type x1, other arithmetic, make_tables(): (jnp.sin(angle) * factor).astype(jnp.bfloat16)  15.8 us
    convert_element_type x1, other arithmetic, make_tables(): (jnp.cos(angle) * factor).astype(jnp.bfloat16)  15.7 us
    all_to_all x2, local copies, waits for them, and re-layouts, local(): lax.all_to_all(adjoint, 'row', split_axis=3, concat_axis=2, tiled=True)  13.1 us
    all_gather x1, waiting for transfers between devices, local(): spectrum_piece = lax.all_gather(stacked, 'row', axis=1, tiled=True)  12.4 us
  transfers between devices with their start and end apart: 4, of which 3 were waited for; matrix products, arithmetic and copies ran while one was open for 20% of the time, Pallas kernels for 0%

commit v1 on v0

--- a/solution.py
+++ b/solution.py
@@ -72,7 +72,7 @@
     field = jnp.stack([field_re, field_im], axis=1)
     power = field[:, 0] * field[:, 0] + field[:, 1] * field[:, 1]
     local_power = jnp.sum(weights[:, None, None] * power, axis=0) / total_points
-    intensity = lax.psum(local_power, "src")
+    intensity = jnp.sum(lax.all_gather(local_power, "src"), axis=0)
     mismatch = intensity - target
     grad_field = (2.0 * weights[:, None, None, None] * mismatch[None, None] * field).astype(
         jnp.bfloat16

time: 506 us -> 432 us (0.85)
  waiting for transfers between devices: 247 us -> 167 us
    psum x1 -> x0, waiting for transfers between devices: 117 us -> none  [local(): intensity = lax.psum(local_power, 'src')]
    all_gather x1, waiting for transfers between devices: 12.4 us -> 40.1 us  [local(): spectrum_piece = lax.all_gather(stacked, 'row', axis=1, tiled=True)]
    all_gather x0 -> x1, waiting for transfers between devices: none -> 11.6 us  [local(): intensity = jnp.sum(lax.all_gather(local_power, 'src'), axis=0)]
  transfers between devices with their start and end apart: 4 -> 4, of which waited for: 3 -> 3; matrix products, arithmetic and copies ran while one was open for 20% -> 25% of each run, Pallas kernels for 0% -> 0%
where the time goes in v1:
time: 432 us; the launch traced here: 431 us
  waiting for transfers between devices  167 us (39%)
  local copies, waits for them, and re-layouts  160 us (37%)
  other arithmetic  44.1 us (10%)
  between operations  29.8 us (7%)
  matrix products  20.4 us (5%)
  starting transfers between devices  9.38 us (2%)
    psum x1, waiting for transfers between devices, local(): grad_re, grad_im = lax.psum((local_re, local_im), 'src')  116 us
    gather x96, local copies, waits for them, and re-layouts  103 us
    all_gather x1, waiting for transfers between devices, local(): spectrum_piece = lax.all_gather(stacked, 'row', axis=1, tiled=True)  40.1 us
    unnamed x22, local copies, waits for them, and re-layouts  24.9 us
    convert_element_type x1, other arithmetic, make_tables(): (jnp.sin(angle) * factor).astype(jnp.bfloat16)  15.8 us
    convert_element_type x1, other arithmetic, make_tables(): (jnp.cos(angle) * factor).astype(jnp.bfloat16)  15.7 us
    all_to_all x2, local copies, waits for them, and re-layouts, local(): lax.all_to_all(adjoint, 'row', split_axis=3, concat_axis=2, tiled=True)  13 us
    all_gather x1, waiting for transfers between devices, local(): intensity = jnp.sum(lax.all_gather(local_power, 'src'), axis=0)  11.6 us
  transfers between devices with their start and end apart: 4, of which 3 were waited for; matrix products, arithmetic and copies ran while one was open for 25% of the time, Pallas kernels for 0%

profile of v1, /device:TPU:1, one launch (start us, length us, event | category | flops | bytes accessed | tf_op | source)
XLA Modules:
  0.0 430.7 jit_solution(12978605900237988577)
XLA Ops:
  9.6 15.8 %multiply_convert_fusion = bf16[1024,1024]{1,0:T(8,128)(2,1)S(1)} fusion(), kind=kLoop, calls=%fused_computation.23 | loop fusion | flops 16777216 | bytes 2097152 | tf_op jit(solution)/shard_map/convert_element_type | solution.py:18
  25.4 15.7 %multiply_convert_fusion.1 = bf16[1024,1024]{1,0:T(8,128)(2,1)S(1)} fusion(), kind=kLoop, calls=%fused_computation.24 | loop fusion | flops 16777216 | bytes 2097152 | tf_op jit(solution)/shard_map/convert_element_type | solution.py:17
  45.3 15.5 %while.9 = (s32[]{:T(128)}, bf16[1024,64]{1,0:T(8,128)(2,1)S(1)}, s32[8,2]{0,1:T(2,128)S(1)}, bf16[8,384,64]{2,1,0:T(8,128)(2,1)}) while((s32[]{:T(128)}, bf16[1024,64]{1,0:T(8,128)(2,1)S(1)}, s32[8,2]{0,1:T(2,128)S(1)}, bf16[8,384,64]{2,1,0:T(8,128)(2,1)}) %tuple.83), condition=%wide.while_cond.1.clone, body=%wide.while_body.1.sunk.clone | while | flops 2 | bytes 148061 | solution.py:52
  60.8 40.1 %all-gather.4.cloned.1.call-done = bf16[2,1024,1024]{2,1,0:T(8,128)(2,1)} async-done(((bf16[2,32,1024]{2,1,0:T(8,128)(2,1)}), bf16[2,1024,1024]{2,1,0:T(8,128)(2,1)}) %all-gather.4.cloned.1.call-update) | async-done | bytes 4194320 | tf_op jit(solution)/shard_map/all_gather | solution.py:55
  100.9 37.9 %while.8 = (s32[]{:T(128)}, bf16[2,1024,1024]{2,1,0:T(8,128)(2,1)}, s32[8,3]{0,1:T(4,128)S(1)}, bf16[8,2,1024,384]{3,2,1,0:T(8,128)(2,1)}) while((s32[]{:T(128)}, bf16[2,1024,1024]{2,1,0:T(8,128)(2,1)}, s32[8,3]{0,1:T(4,128)S(1)}, bf16[8,2,1024,384]{3,2,1,0:T(8,128)(2,1)}) %tuple.80), condition=%wide.while_cond.clone, body=%wide.while_body.sunk.clone | while | flops 2 | bytes 3146341 | solution.py:57
  101.5 4.2 bitcast_dynamic-update-slice_fusion.12
  106.3 4.2 bitcast_dynamic-update-slice_fusion.12
  111.0 4.2 bitcast_dynamic-update-slice_fusion.12
  115.8 4.2 bitcast_dynamic-update-slice_fusion.12
  120.5 4.1 bitcast_dynamic-update-slice_fusion.12
  129.9 4.2 bitcast_dynamic-update-slice_fusion.12
  134.7 4.2 bitcast_dynamic-update-slice_fusion.12
  138.9 7.9 %fusion = f32[8,2,1024,64]{2,3,1,0:T(8,128)S(1)} fusion(bf16[8,2,1024,384]{3,2,1,0:T(8,128)(2,1)} %get-tuple-element.9, pred[8,1024,384]{2,1,0:T(8,128)(4,1)} %add_compare_fusion, bf16[8,384,64]{2,1,0:T(8,128)(2,1)} %get-tuple-element.17), kind=kOutput, calls=%fused_computation.9 | convolution fusion | flops 811597824 | bytes 20316160 | tf_op jit(solution)/shard_map/pckl,plz->pckz/dot_general | solution.py:61
  156.3 29.4 %while.11 = (s32[]{:T(128)}, bf16[1024,1024]{1,0:T(8,128)(2,1)}, s32[8,2]{0,1:T(2,128)S(1)}, bf16[8,1024,384]{2,1,0:T(8,128)(2,1)}) while((s32[]{:T(128)}, bf16[1024,1024]{1,0:T(8,128)(2,1)}, s32[8,2]{0,1:T(2,128)S(1)}, bf16[8,1024,384]{2,1,0:T(8,128)(2,1)}) %tuple.100), condition=%wide.while_cond.3.clone, body=%wide.while_body.3.sunk.clone | while | flops 2 | bytes 1573469 | solution.py:93
  185.7 11.6 %all-gather.6.cloned.1.call-done = f32[512,1024]{1,0:T(8,128)} async-done(((f32[32,1024]{1,0:T(8,128)}), f32[512,1024]{1,0:T(8,128)}) %all-gather.6.cloned.1.call-update) | async-done | bytes 2097168 | tf_op jit(solution)/shard_map/all_gather | solution.py:75
  199.2 4.3 fusion.11
  204.0 7.5 %copy.18 = bf16[8,2,32,1024]{2,1,0,3:T(2,128)(2,1)} copy(bf16[8,2,32,1024]{3,2,1,0:T(8,128)(2,1)S(1)} %pad_maximum_fusion) | data formatting | bytes 2097152 | tf_op jit(solution)/shard_map/stack | solution.py:85
  211.5 9.9 %reshape.202 = bf16[32,2,8192]{2,1,0:T(2,128)(2,1)} reshape(bf16[1024,8,2,32]{3,2,1,0:T(2,128)(2,1)} %bitcast.160) | data formatting | bytes 2097152
  221.4 9.3 %all-to-all-start = ((bf16[32,2,8192]{2,1,0:T(2,128)(2,1)}), bf16[32,2,8192]{2,1,0:T(2,128)(2,1)S(1)}, u32[]{:S(2)}, u32[]{:S(2)}) async-start(bf16[32,2,8192]{2,1,0:T(2,128)(2,1)} %reshape.202), calls=%async_computation | async-start | bytes 2097152 | tf_op jit(solution)/shard_map/all_to_all | solution.py:86
  250.2 19.9 %while.10 = (s32[]{:T(128)}, bf16[1024,1024]{1,0:T(8,128)(2,1)S(1)}, s32[8,2]{0,1:T(2,128)S(1)}, bf16[8,1024,384]{2,1,0:T(8,128)(2,1)}) while((s32[]{:T(128)}, bf16[1024,1024]{1,0:T(8,128)(2,1)S(1)}, s32[8,2]{0,1:T(2,128)S(1)}, bf16[8,1024,384]{2,1,0:T(8,128)(2,1)}) %tuple.101), condition=%wide.while_cond.2.clone, body=%wide.while_body.2.sunk.clone | while | flops 2 | bytes 1573469 | solution.py:92
  273.6 6.8 %copy.30 = bf16[8,2,32,32,32]{2,3,4,1,0:T(8,128)(2,1)} copy(bf16[8,2,32,32,32]{2,1,0,4,3:T(2,128)(2,1)} %bitcast.161) | data formatting | bytes 2097152 | tf_op jit(solution)/shard_map/all_to_all | solution.py:86
  280.5 6.2 %all_to_all.16 = bf16[8,2,1024,32]{2,3,1,0:T(8,128)(2,1)S(1)} reshape(bf16[8,2,32,32,32]{3,2,4,1,0:T(8,128)(2,1)} %bitcast.162) | data formatting | bytes 2097152 | tf_op jit(solution)/shard_map/all_to_all | solution.py:86
  286.6 5.9 %fusion.2 = f32[8,2,32,768]{3,2,1,0:T(8,128)S(1)} fusion(bf16[8,2,1024,32]{2,3,1,0:T(8,128)(2,1)S(1)} %all_to_all.16, bf16[8,1024,384]{2,1,0:T(8,128)(2,1)} %get-tuple-element.33, bf16[8,1024,384]{2,1,0:T(8,128)(2,1)} %get-tuple-element.25), kind=kOutput, calls=%fused_computation.12 | convolution fusion | flops 830472192 | bytes 15204352 | tf_op jit(solution)/shard_map/pcyk,pyz->pckz/dot_general | solution.py:98
  305.4 115.6 %all-reduce.6.cloned.1.call-done = (f32[32,1024]{1,0:T(8,128)}, f32[32,1024]{1,0:T(8,128)}) async-done(((f32[32,1024]{1,0:T(8,128)}, f32[32,1024]{1,0:T(8,128)}), (f32[32,1024]{1,0:T(8,128)}, f32[32,1024]{1,0:T(8,128)})) %all-reduce.6.cloned.1.call-update) | async-done | bytes 262160 | tf_op jit(solution)/shard_map/psum | solution.py:113
  (176 shorter events, 115.1 us)
Async XLA Ops:
  7.2 34.4 %copy-start.7 = (s32[8]{0:T(128)S(1)}, s32[8]{0:T(128)}, u32[]{:S(2)}) copy-start(s32[8]{0:T(128)} %param.11) | copy-start | bytes 100
  7.2 34.5 %copy-start.5 = (s32[8]{0:T(128)S(1)}, s32[8]{0:T(128)}, u32[]{:S(2)}) copy-start(s32[8]{0:T(128)} %param.10) | copy-start | bytes 100
  7.2 93.8 %all-gather.4.cloned.1.call-start = ((), (), s32[]{:S(2)}) async-start(), calls=%async_computation.1 | async-start | bytes 4325376 | tf_op jit(solution)/shard_map/all_gather | solution.py:55
  8.8 188.5 %all-gather.6.cloned.1.call-start = ((), (), s32[]{:S(2)}) async-start(), calls=%async_computation.2 | async-start | bytes 2228224 | tf_op jit(solution)/shard_map/all_gather | solution.py:75
  25.4 15.7 %copy-start = (bf16[1024,1024]{1,0:T(8,128)(2,1)}, bf16[1024,1024]{1,0:T(8,128)(2,1)S(1)}, u32[]{:S(2)}) copy-start(bf16[1024,1024]{1,0:T(8,128)(2,1)S(1)} %multiply_convert_fusion) | copy-start | bytes 6291460
  146.7 1.6 copy-start.1
  148.3 2.4 copy-start.6
  156.3 42.8 %copy-start.4 = (f32[32,1024]{1,0:T(8,128)S(1)}, f32[32,1024]{1,0:T(8,128)}, u32[]{:S(2)}) copy-start(f32[32,1024]{1,0:T(8,128)} %param.8) | copy-start | bytes 393220
  221.4 48.6 %all-to-all-start = ((bf16[32,2,8192]{2,1,0:T(2,128)(2,1)}), bf16[32,2,8192]{2,1,0:T(2,128)(2,1)S(1)}, u32[]{:S(2)}, u32[]{:S(2)}) async-start(bf16[32,2,8192]{2,1,0:T(2,128)(2,1)} %reshape.202), calls=%async_computation | async-start | bytes 2097152 | tf_op jit(solution)/shard_map/all_to_all | solution.py:86
  230.7 190.3 %all-reduce.6.cloned.1.call-start = ((), (), s32[]{:S(2)}) async-start(), calls=%async_computation.3 | async-start | bytes 524288 | tf_op jit(solution)/shard_map/psum | solution.py:113
  298.7 6.1 %copy-start.3 = (f32[32,1024]{1,0:T(8,128)}, f32[32,1024]{1,0:T(8,128)S(1)}, u32[]{:S(2)}) copy-start(f32[32,1024]{1,0:T(8,128)S(1)} %dynamic_update_slice.55) | copy-start | bytes 393220
  304.7 0.7 copy-start.2
Sparse Core Ops, SparseCore 0:
  11.7 89.1 all-gather.3
  153.1 44.1 all-gather.5
  305.6 115.4 all-reduce.5
